TPU v7x, 512 devices: a whole 4x4x16 slice. The times are simulated.
512 devices in a mesh: batch: 16 (over z), token: 32 (over x, y, core).
Axes of the slice: x: 4, y: 4, z: 16, core: 2. Of those that a mesh axis runs over, the one named last changes fastest.
Arguments:
- tokens: bfloat16 [262144, 768], P(('batch', 'token')), may hold values from -9 to 9
- slot_weight: bfloat16 [768, 1024], replicated, may hold values from -2 to 2
- expert_in: bfloat16 [128, 768, 3072], P('token', None, 'batch'), may hold values from -1.7265625 to 1.7265625
- expert_out: bfloat16 [128, 3072, 768], P('token', 'batch'), may hold values from -0.6484375 to 0.6484375
Outputs:
- mixed: bfloat16 [262144, 768], P(('batch', 'token'))
All inputs are finite; a program needn't handle non-finite values.
Results may differ from a plain program's by a relative error of at most 0.023.
Values may be sent and summed in bfloat16 or wider, within the bound.
A program may use at most 64 MiB of HBM per device.

v0:
```python
import jax
import jax.numpy as jnp
from jax import lax
from jax.sharding import Mesh
from jax.sharding import PartitionSpec as P

TOKEN = ("token_0", "token_1", "token_2")
BATCH_TOKEN = ("batch", "token_0", "token_1", "token_2")


def gathered_once(shard, axis):
    leaves = jax.tree.leaves(shard)
    order = sorted(range(len(leaves)), key=lambda k: -leaves[k].size)
    width = (1, *leaves[order[0]].shape)[-1]
    lines = [
        jnp.pad(leaves[k].reshape(-1), (0, -leaves[k].size % width)).reshape(-1, width)
        for k in order
    ]
    both, at, found = (lax.all_gather(jnp.concatenate(lines), axis), 0, {})
    for k, line in zip(order, lines):
        section = both[:, at : at + len(line)].reshape(len(both), -1)
        found[k] = section[:, : leaves[k].size].reshape(-1, *leaves[k].shape)
        at += len(line)
    numbers = iter(range(len(leaves)))
    return jax.tree.map(lambda _: found[next(numbers)], shard)


def merged_by_axis(shard, axes, combine):
    for axis in axes:
        pieces = gathered_once(shard, axis)
        shard = jax.tree.map(lambda part: part[0], pieces)
        for k in range(1, lax.axis_size(axis)):
            shard = combine(shard, jax.tree.map(lambda part: part[k], pieces))
    return shard


def split_up(shard, dim, length):
    dims = shard.shape
    blocks = shard.reshape(*dims[:dim], length, dims[dim] // length, *dims[dim + 1 :])
    return jnp.moveaxis(blocks, dim, 0)


def sent_and_summed(shard, axis, dim):
    blocks = split_up(shard, dim, lax.axis_size(axis))
    arrived = lax.all_to_all(blocks, axis, split_axis=0, concat_axis=0, tiled=True)
    return arrived.astype(jnp.float32).sum(axis=0)


def in_order(blocks, dim):
    blocks = jnp.moveaxis(blocks, 0, dim)
    dims = blocks.shape
    return blocks.reshape(*dims[:dim], dims[dim] * dims[dim + 1], *dims[dim + 2 :])


def from_everyone(shard, axis):
    copies = jnp.broadcast_to(shard, (lax.axis_size(axis), *shard.shape))
    return lax.all_to_all(copies, axis, split_axis=0, concat_axis=0, tiled=True)


def gathered_copies(shard, axis, dim):
    return in_order(from_everyone(shard, axis), dim)


def join_stats(former, latter):
    highest = jnp.maximum(former[0], latter[0])
    total = former[1] * jnp.exp(former[0] - highest) + latter[1] * jnp.exp(latter[0] - highest)
    return (highest, total)


def body(tokens, slot_weight, expert_in, expert_out):
    widened = tokens.astype(jnp.float32)
    scale_row = lax.rsqrt(jnp.mean(widened * widened, axis=-1, keepdims=True) + 1e-06)
    normed = (widened * scale_row).astype(jnp.bfloat16)
    logits = jnp.dot(normed, slot_weight, preferred_element_type=jnp.float32)
    local_max = jnp.max(logits, axis=0)
    local_sum = jnp.sum(jnp.exp(logits - local_max[None, :]), axis=0)
    column_max, column_sum = merged_by_axis((local_max, local_sum), TOKEN, join_stats)
    raised = jnp.exp(logits - column_max[None, :])
    dispatch = raised.astype(jnp.bfloat16)
    partial_value = jnp.einsum("ts,td->sd", dispatch, normed, preferred_element_type=jnp.float32)
    own_count = slot_weight.shape[1] // lax.axis_size(TOKEN)
    offset = lax.axis_index(TOKEN) * own_count
    own_rows = sent_and_summed(partial_value.astype(jnp.bfloat16), TOKEN, 0)
    own_total = lax.dynamic_slice_in_dim(column_sum, offset, own_count, 0)
    experts_here = expert_in.shape[0]
    slot_inputs = (own_rows / own_total[:, None]).astype(jnp.bfloat16)
    slot_inputs = slot_inputs.reshape(experts_here, own_count // experts_here, tokens.shape[1])
    hidden = jnp.einsum(
        "esd,edf->esf",
        lax.all_gather(slot_inputs, "batch", axis=1, tiled=True),
        expert_in,
        preferred_element_type=jnp.float32,
    )
    hidden = jax.nn.gelu(hidden, approximate=False).astype(jnp.bfloat16)
    terms = jnp.einsum("esf,efd->esd", hidden, expert_out, preferred_element_type=jnp.float32)
    slot_outputs = sent_and_summed(terms.astype(jnp.bfloat16), "batch", 1).astype(jnp.bfloat16)
    combine = jax.nn.softmax(logits, axis=1).astype(jnp.bfloat16)
    slots_each = slot_outputs.shape[1]
    block_rows = gathered_copies(slot_outputs, TOKEN, 0)
    number = block_rows.shape[0]
    flat_rows = block_rows.reshape(number * slots_each, block_rows.shape[2])
    mixed = jnp.dot(combine, flat_rows, preferred_element_type=jnp.float32)
    return mixed.astype(jnp.bfloat16)


def solution(mesh):
    torus = Mesh(
        mesh.devices.reshape(mesh.shape["batch"], 4, 4, 2),
        ("batch", "token_0", "token_1", "token_2"),
    )
    placed = (P(BATCH_TOKEN, None), P(), P(TOKEN, None, "batch"), P(TOKEN, "batch", None))
    return jax.shard_map(
        body, mesh=torus, in_specs=placed, out_specs=P(BATCH_TOKEN, None), check_vma=False
    )
```

profile of v0, /device:TPU:1, one launch (start us, length us, event | category | flops | bytes accessed | tf_op | source)
XLA Modules:
  0.0 176.2 jit_solution(4309130232594882701)
XLA Ops:
  0.0 0.0 copy-start
  0.0 1.5 fusion.1
  1.5 0.2 copy-done
  1.6 2.3 %fusion.110 = (f32[512]{0:T(512)S(1)}, f32[1024]{0:T(1024)S(1)}, f32[512,1024]{1,0:T(8,128)S(1)}) fusion(bf16[768,1024]{1,0:T(8,128)(2,1)S(1)} %copy-done, bf16[512,768]{1,0:T(8,128)(2,1)} %param.4, f32[512]{0:T(512)S(1)} %add_rsqrt_fusion), kind=kOutput, calls=%fused_computation.153 | convolution fusion | flops 807533056 | bytes 4464640 | tf_op jit(solution)/shard_map/dot_general | solution.py:74
  3.9 0.0 copy-start.1
  3.9 0.0 copy-start.3
  3.9 0.7 fusion
  4.7 10.3 %all-gather.3 = f32[4,2,1024]{2,1,0:T(2,128)S(1)} all-gather(f32[1,2,1024]{2,1,0:T(2,128)S(1)} %maximum_bitcast_fusion), channel_id=2, replica_groups=mesh['batch'=16,'token_0'=4,'token_1'=4,'token_2'=2] {'token_0'}, dimensions={0}, use_global_device_ids=true | all-gather | bytes 40960 | tf_op jit(solution)/shard_map/all_gather | solution.py:19
  15.0 0.1 fusion.65
  15.1 9.6 %all-gather.4 = f32[4,2,1024]{2,1,0:T(2,128)S(1)} all-gather(f32[1,2,1024]{2,1,0:T(2,128)S(1)} %maximum_bitcast_fusion.1), channel_id=3, replica_groups=mesh['batch'=16,'token_0'=4,'token_1'=4,'token_2'=2] {'token_1'}, dimensions={0}, use_global_device_ids=true | all-gather | bytes 40960 | tf_op jit(solution)/shard_map/all_gather | solution.py:19
  24.6 0.1 fusion.56
  24.7 12.4 %all-gather.5 = f32[2,2,1024]{2,1,0:T(2,128)S(1)} all-gather(f32[1,2,1024]{2,1,0:T(2,128)S(1)} %maximum_bitcast_fusion.2), channel_id=4, replica_groups=mesh['batch'=16,'token_0'=4,'token_1'=4,'token_2'=2] {'token_2'}, dimensions={0}, use_global_device_ids=true | all-gather | bytes 24576 | tf_op jit(solution)/shard_map/all_gather | solution.py:19
  37.1 0.0 copy-done.3
  37.1 2.3 %convolution_convert_fusion = bf16[1024,768]{1,0:T(8,128)(2,1)} fusion(f32[512,1024]{1,0:T(8,128)S(1)} %get-tuple-element.21, f32[1024]{0:T(1024)S(1)} %get-tuple-element.12, bf16[512,768]{1,0:T(8,128)(2,1)S(1)} %copy-done.3, f32[512]{0:T(512)S(1)} %add_rsqrt_fusion), kind=kOutput, calls=%fused_computation.8 | convolution fusion | flops 808321024 | bytes 4462592 | tf_op jit(solution)/shard_map/ts,td->sd/dot_general | solution.py:80
  39.4 0.0 copy-done.1
  39.4 4.1 %all-to-all-start = ((bf16[32,32,768]{2,1,0:T(8,128)(2,1)}), bf16[32,32,768]{2,1,0:T(8,128)(2,1)S(1)}, u32[]{:S(2)}, u32[]{:S(2)}) async-start(bf16[32,32,768]{2,1,0:T(8,128)(2,1)} %bitcast.173), calls=%async_computation | async-start | bytes 3145728 | tf_op jit(solution)/shard_map/all_to_all | solution.py:45
  43.6 0.1 dynamic_slice.3
  43.6 0.1 div.29
  43.7 22.5 %all-to-all-done = bf16[32,32,768]{2,1,0:T(8,128)(2,1)S(1)} async-done(((bf16[32,32,768]{2,1,0:T(8,128)(2,1)}), bf16[32,32,768]{2,1,0:T(8,128)(2,1)S(1)}, u32[]{:S(2)}, u32[]{:S(2)}) %all-to-all-start) | async-done | bytes 1572896 | tf_op jit(solution)/shard_map/all_to_all | solution.py:45
  66.2 0.0 copy-start.4
  66.2 0.2 convert_reduce_fusion
  66.4 0.1 fusion.50
  66.5 30.6 %all_gather.27 = bf16[4,128,768]{2,1,0:T(8,128)(2,1)S(1)} all-gather(bf16[4,8,768]{2,1,0:T(8,128)(2,1)S(1)} %fusion.50), channel_id=1, replica_groups=mesh['batch'=16,'token_0'=4,'token_1'=4,'token_2'=2] {'batch'}, dimensions={1}, use_global_device_ids=true | all-gather | bytes 835584 | tf_op jit(solution)/shard_map/all_gather | solution.py:90
  97.2 0.0 copy-done.4
  97.2 0.0 copy-start.5
  97.2 0.5 fusion.52
  97.7 0.8 copy-done.5
  98.4 1.2 fusion.3
  99.6 0.1 copy.7
  99.7 36.1 %all_to_all.15 = bf16[16,4,8,768]{3,2,1,0:T(8,128)(2,1)S(1)} all-to-all(bf16[16,4,8,768]{3,2,1,0:T(8,128)(2,1)S(1)} %bitcast.172), channel_id=1, replica_groups=mesh['batch'=16,'token_0'=4,'token_1'=4,'token_2'=2] {'batch'}, dimensions={0} | all-to-all | bytes 1572864 | tf_op jit(solution)/shard_map/all_to_all | solution.py:45
  135.8 0.1 reduce_sum.55
  136.0 0.2 broadcast_in_dim.2
  136.1 0.0 copy-start.2
  136.1 38.0 %all_to_all.16 = bf16[32,4,8,768]{3,2,1,0:T(8,128)(2,1)S(1)} all-to-all(bf16[32,4,8,768]{3,2,1,0:T(8,128)(2,1)S(1)} %broadcast_in_dim.2), channel_id=1, replica_groups=mesh['batch'=16,'token_0'=4,'token_1'=4,'token_2'=2] {'token_0','token_1..., dimensions={0} | all-to-all | bytes 3145728 | tf_op jit(solution)/shard_map/all_to_all | solution.py:57
  174.2 0.0 copy-done.2
  174.2 2.0 %convolution_convert_fusion.1 = bf16[512,768]{1,0:T(8,128)(2,1)} fusion(bf16[1024,768]{1,0:T(8,128)(2,1)S(1)} %bitcast.174, f32[512,1024]{1,0:T(8,128)S(1)} %copy-done.2, f32[512]{0:T(512)S(1)} %get-tuple-element.5, f32[512]{0:T(512)S(1)} %get-tuple-element.7), kind=kOutput, calls=%fused_computation.11 | convolution fusion | flops 807272448 | bytes 4460544 | tf_op jit(solution)/shard_map/dot_general | solution.py:102
  (6 shorter events, 0.1 us)
Async XLA Ops:
  0.0 1.6 copy-start
  3.9 35.5 %copy-start.1 = (f32[512,1024]{1,0:T(8,128)}, f32[512,1024]{1,0:T(8,128)S(1)}, u32[]{:S(2)}) copy-start(f32[512,1024]{1,0:T(8,128)S(1)} %get-tuple-element.21) | copy-start | bytes 6291460
  3.9 33.2 %copy-start.3 = (bf16[512,768]{1,0:T(8,128)(2,1)S(1)}, bf16[512,768]{1,0:T(8,128)(2,1)}, u32[]{:S(2)}) copy-start(bf16[512,768]{1,0:T(8,128)(2,1)} %param.4) | copy-start | bytes 2359300
  39.4 26.8 %all-to-all-start = ((bf16[32,32,768]{2,1,0:T(8,128)(2,1)}), bf16[32,32,768]{2,1,0:T(8,128)(2,1)S(1)}, u32[]{:S(2)}, u32[]{:S(2)}) async-start(bf16[32,32,768]{2,1,0:T(8,128)(2,1)} %bitcast.173), calls=%async_computation | async-start | bytes 3145728 | tf_op jit(solution)/shard_map/all_to_all | solution.py:45
  66.2 30.9 %copy-start.4 = (bf16[4,768,192]{1,2,0:T(8,128)(2,1)S(1)}, bf16[4,768,192]{1,2,0:T(8,128)(2,1)}, u32[]{:S(2)}) copy-start(bf16[4,768,192]{1,2,0:T(8,128)(2,1)} %param.6) | copy-start | bytes 3538948
  97.2 1.3 copy-start.5
  136.1 38.0 %copy-start.2 = (f32[512,1024]{1,0:T(8,128)S(1)}, f32[512,1024]{1,0:T(8,128)}, u32[]{:S(2)}) copy-start(f32[512,1024]{1,0:T(8,128)} %copy-done.1) | copy-start | bytes 6291460
where the time goes:
time: 177 us; the launch traced here: 176 us
  blocking collectives  137 us (77%)
  waiting for transfers between devices  22.5 us (13%)
  matrix products  8.2 us (5%)
  starting transfers between devices  4.14 us (2%)
  other arithmetic  2.79 us (2%)
    all_to_all x1, blocking collectives, from_everyone(): return lax.all_to_all(copies, axis, split_axis=0, concat_axis=0, tiled=True)  38 us
    all_to_all x1, blocking collectives, sent_and_summed(): lax.all_to_all(blocks, axis, split_axis=0, concat_axis=0, tiled=True)  36.1 us
    all_gather x3, blocking collectives, gathered_once(): both, at, found = (lax.all_gather(jnp.concatenate(lines), axis), 0, {})  32.3 us
    all_gather x1, blocking collectives, body(): lax.all_gather(slot_inputs, 'batch', axis=1, tiled=True)  30.6 us
    all_to_all x1, waiting for transfers between devices, sent_and_summed(): lax.all_to_all(blocks, axis, split_axis=0, concat_axis=0, tiled=True)  22.5 us
    all_to_all x1, starting transfers between devices, sent_and_summed(): lax.all_to_all(blocks, axis, split_axis=0, concat_axis=0, tiled=True)  4.14 us
  transfers between devices with their start and end apart: 1, of which 1 were waited for; matrix products, arithmetic and copies ran while one was open for 0% of the time, Pallas kernels for 0%

commit v1 on v0

v1 whole, which is shorter than its diff:
```python
import functools

import jax
import jax.numpy as jnp
from jax import lax
from jax.experimental import pallas as pl
from jax.experimental.pallas import tpu as pltpu
from jax.sharding import Mesh
from jax.sharding import PartitionSpec as P

GRID = pl.DeviceIdType.MESH
F32 = jnp.float32
BF16 = jnp.bfloat16
LANES = 128


def layer(
    sizes,
    tokens_hbm,
    slot_hbm,
    first_hbm,
    second_hbm,
    mixed_hbm,
    tok,
    wv,
    w1,
    w2,
    nrm,
    lg,
    lo,
    dsp,
    part,
    st,
    rb,
    sr,
    vv,
    xin,
    tt,
    dsl,
    dsr,
    drl,
    drr,
    gg,
    cb,
    rinv,
    outv,
    load_sem,
    out_sem,
    tok_sem,
    st_send,
    st_recv,
    pb_send,
    pb_recv,
    c_send,
    c_recv,
    d_send,
    d_recv,
    e_send,
    e_recv,
    f_send,
    f_recv,
):
    nz, nx, ny = sizes
    z, x, y, c = (lax.axis_index(a) for a in ("z", "x", "y", "c"))
    T, D = tokens_hbm.shape
    S = slot_hbm.shape[1]
    H = S // 2
    E = first_hbm.shape[0]
    chips = nx * ny
    R = S // (2 * chips)
    RE = R // E
    xh_n = nx // 2
    kr = nz // 2
    kl = kr - 1
    me = x * ny + y
    half_rows = R // 2
    sibling = {"c": 1 - c}
    right = {"z": lax.rem(z + 1, nz)}
    left = {"z": lax.rem(z + nz - 1, nz)}

    barrier = pltpu.get_barrier_semaphore()
    peers = 2

    def greet(dev):
        pl.semaphore_signal(barrier, inc=1, device_id=dev, device_id_type=GRID)

    greet(right)
    greet(left)
    for dx in range(nx):
        for dy in range(ny):
            for dc in range(2):
                if dx or dy or dc:
                    greet(
                        {
                            "x": lax.rem(x + dx, nx),
                            "y": lax.rem(y + dy, ny),
                            "c": lax.rem(c + dc, 2),
                        }
                    )
                    peers += 1

    own_cols = pl.ds(pl.multiple_of(c * H, LANES), H)
    other_cols = pl.ds(pl.multiple_of((1 - c) * H, LANES), H)
    loads = [
        pltpu.make_async_copy(tokens_hbm, tok, load_sem.at[0]),
        pltpu.make_async_copy(slot_hbm.at[:, own_cols], wv.at[0], load_sem.at[1]),
        pltpu.make_async_copy(slot_hbm.at[:, other_cols], wv.at[1], load_sem.at[2]),
        pltpu.make_async_copy(first_hbm, w1, load_sem.at[3]),
        pltpu.make_async_copy(second_hbm, w2, load_sem.at[4]),
    ]
    for load in loads:
        load.start()

    chunk = min(256, T)

    loads[0].wait()

    def normalize(i, _):
        rows = pl.ds(pl.multiple_of(i * 64, 64), 64)
        wide = tok[rows, :].astype(F32)
        mean = jnp.mean(wide * wide, axis=-1, keepdims=True)
        nrm[rows, :] = (wide * lax.rsqrt(mean + 1e-6)).astype(BF16)
        return 0

    lax.fori_loop(0, T // 64, normalize, 0)

    pl.semaphore_wait(barrier, peers)

    swap = pltpu.make_async_remote_copy(
        src_ref=nrm.at[pl.ds(0, T)],
        dst_ref=nrm.at[pl.ds(T, T)],
        send_sem=tok_sem.at[0],
        recv_sem=tok_sem.at[1],
        device_id=sibling,
        device_id_type=GRID,
    )
    swap.start()

    loads[1].wait()
    loads[2].wait()
    for i in range(T // chunk):
        rows = pl.ds(i * chunk, chunk)
        lg[rows, :] = jnp.dot(nrm[rows, :], wv[0], preferred_element_type=F32)
        lo[rows, :] = jnp.dot(nrm[rows, :], wv[1], preferred_element_type=F32)
    swap.wait_recv()
    for i in range(T // chunk):
        rows = pl.ds(T + i * chunk, chunk)
        lg[rows, :] = jnp.dot(nrm[rows, :], wv[0], preferred_element_type=F32)

    step_rows = 64

    def highest(i, best):
        rows = pl.ds(pl.multiple_of(i * step_rows, step_rows), step_rows)
        block = lg[rows, :].reshape(step_rows // 8, 8, H)
        return jnp.maximum(best, jnp.max(block, axis=0))

    best = lax.fori_loop(0, 2 * T // step_rows, highest, jnp.full((8, H), -jnp.inf, F32))
    column_max = jnp.max(best, axis=0, keepdims=True)

    def raise_rows(i, total):
        rows = pl.ds(pl.multiple_of(i * step_rows, step_rows), step_rows)
        raised = jnp.exp(lg[rows, :] - column_max)
        dsp[rows, :] = raised.astype(BF16)
        return total + jnp.sum(raised.reshape(step_rows // 8, 8, H), axis=0)

    total = lax.fori_loop(0, 2 * T // step_rows, raise_rows, jnp.zeros((8, H), F32))
    column_sum = jnp.sum(total, axis=0, keepdims=True)
    for j in range(H // LANES):
        cols = slice(j * LANES, (j + 1) * LANES)
        st[j, 0:1, :] = column_max[:, cols]
        st[j, 1:2, :] = column_sum[:, cols]

    def targets():
        for xh in range(xh_n):
            for yt in range(ny):
                for ct in range(2):
                    yield xh, yt, ct, (xh * ny + yt) * 2 + ct

    def to_owner(xh, yt, ct, number, what):
        xt = xh_n * c + xh
        row = number * R
        if what == "stat":
            src, dst = st.at[row // LANES], sr.at[me]
            ssem, rsem = st_send.at[number], st_recv.at[me]
        else:
            src, dst = part.at[pl.ds(row, R)], rb.at[me]
            ssem, rsem = pb_send.at[number], pb_recv.at[me]
        here = (xt == x) & (yt == y) & (ct == c)
        far = pltpu.make_async_remote_copy(
            src_ref=src,
            dst_ref=dst,
            send_sem=ssem,
            recv_sem=rsem,
            device_id={"x": xt, "y": yt, "c": ct},
            device_id_type=GRID,
        )
        near = pltpu.make_async_copy(src, dst, rsem)
        return here, far, near

    def start_owner(*args):
        here, far, near = to_owner(*args)
        pl.when(jnp.logical_not(here))(far.start)
        pl.when(here)(near.start)

    for xh, yt, ct, number in targets():
        start_owner(xh, yt, ct, number, "stat")

    block = ny * 2 * R
    for xh in range(xh_n):
        value = lax.dot_general(
            dsp[:, xh * block : (xh + 1) * block],
            nrm[...],
            (((0,), (0,)), ((), ())),
            preferred_element_type=F32,
        )
        part[xh * block : (xh + 1) * block, :] = value.astype(BF16)
        for yt in range(ny):
            for ct in range(2):
                start_owner(xh, yt, ct, (xh * ny + yt) * 2 + ct, "part")

    def combine_rows(i, _):
        rows = pl.ds(pl.multiple_of(i * 32, 32), 32)
        one, two = lg[rows, :], lo[rows, :]
        top = jnp.maximum(
            jnp.max(one, axis=1, keepdims=True), jnp.max(two, axis=1, keepdims=True)
        )
        one, two = jnp.exp(one - top), jnp.exp(two - top)
        cb[0, rows, :] = one.astype(BF16)
        cb[1, rows, :] = two.astype(BF16)
        weight = jnp.sum(one, axis=1, keepdims=True) + jnp.sum(two, axis=1, keepdims=True)
        rinv[rows, :] = jnp.broadcast_to(1.0 / weight, (32, LANES))
        return 0

    lax.fori_loop(0, T // 32, combine_rows, 0)

    def arrived(buf, sem, q):
        return pltpu.make_async_remote_copy(
            src_ref=buf.at[q],
            dst_ref=buf.at[q],
            send_sem=sem.at[q],
            recv_sem=sem.at[q],
            device_id=sibling,
            device_id_type=GRID,
        )

    for q in range(chips):
        arrived(sr, st_recv, q).wait_recv()
    tops = [sr[q, 0:1, :] for q in range(chips)]
    peak = functools.reduce(jnp.maximum, tops)
    weights = [jnp.exp(t - peak) for t in tops]
    sums = functools.reduce(jnp.add, [w * sr[q, 1:2, :] for q, w in enumerate(weights)])
    vv[...] = jnp.zeros_like(vv)
    for q in range(chips):
        vv[q : q + 1, :] = weights[q] / sums
    vv[...] = jnp.transpose(vv[...])
    offset = lax.rem((lax.rem(x, xh_n) * ny + y) * 2 * R + c * R, LANES)
    scale = vv[pl.ds(pl.multiple_of(offset, R), R), :]
    acc = jnp.zeros((R, D), F32)
    for q in range(chips):
        arrived(rb, pb_recv, q).wait_recv()
        acc = acc + scale[:, q : q + 1] * rb[q].astype(F32)
    xin[0] = acc.astype(BF16)

    def halves(ref, i, h):
        return ref.at[i, pl.ds(h * half_rows, half_rows)]

    def pass_on(slot, h, dev, to):
        return pltpu.make_async_remote_copy(
            src_ref=halves(xin, slot, h),
            dst_ref=halves(xin, to, h),
            send_sem=c_send.at[to, h],
            recv_sem=c_recv.at[to, h],
            device_id=dev,
            device_id_type=GRID,
        )

    for h in range(2):
        pass_on(0, h, right, 1).start()
        if kl:
            pass_on(0, h, left, kr + 1).start()

    loads[3].wait()
    loads[4].wait()

    def experts(a, b):
        rows_a, rows_b = xin[a].astype(F32), xin[b].astype(F32)
        for e in range(E):
            part_e = slice(e * RE, (e + 1) * RE)
            rows = jnp.concatenate([rows_a[part_e], rows_b[part_e]], axis=0).astype(BF16)
            hidden = lax.dot_general(
                rows, w1[e], (((1,), (1,)), ((), ())), preferred_element_type=F32
            )
            hidden = 0.5 * hidden * (1.0 + lax.erf(hidden * (0.5**0.5)))
            terms = jnp.dot(hidden.astype(BF16), w2[e], preferred_element_type=F32)
            tt[a, pl.ds(e * RE, RE), :] = terms[:RE]
            tt[b, pl.ds(e * RE, RE), :] = terms[RE:]

    def gather_step(k, _):
        for h in range(2):
            pass_on(0, h, right, k).wait_recv()

            @pl.when(k < kr)
            def _():
                pass_on(k, h, right, k + 1).start()

            @pl.when(k <= kl)
            def _():
                pass_on(0, h, left, kr + k).wait_recv()

            @pl.when(k < kl)
            def _():
                pass_on(kr + k, h, left, kr + k + 1).start()

        experts(k, jnp.where(k < kr, kr + k, 0))
        return 0

    lax.fori_loop(1, kr + 1, gather_step, 0)

    def hand_back(k, h, way):
        src, dst, dev = ((dsl, drl, left), (dsr, drr, right))[way]
        return pltpu.make_async_remote_copy(
            src_ref=halves(src, k, h),
            dst_ref=halves(dst, k - 1, h),
            send_sem=d_send.at[way, k, h],
            recv_sem=d_recv.at[way, k - 1, h],
            device_id=dev,
            device_id_type=GRID,
        )

    def return_step(i, _):
        k = kr - i
        for h in range(2):
            rows = pl.ds(h * half_rows, half_rows)

            @pl.when(k == kr)
            def _():
                dsl[k, rows, :] = tt[k, rows, :].astype(BF16)

            @pl.when(k < kr)
            def _():
                hand_back(k + 1, h, 0).wait_recv()
                dsl[k, rows, :] = (tt[k, rows, :] + drl[k, rows, :].astype(F32)).astype(BF16)

            hand_back(k, h, 0).start()

            @pl.when(k == kl)
            def _():
                dsr[k, rows, :] = tt[kr + k, rows, :].astype(BF16)

            @pl.when(k < kl)
            def _():
                hand_back(k + 1, h, 1).wait_recv()
                dsr[k, rows, :] = (tt[kr + k, rows, :] + drr[k, rows, :].astype(F32)).astype(BF16)

            @pl.when(k <= kl)
            def _():
                hand_back(k, h, 1).start()

        return 0

    lax.fori_loop(0, kr, return_step, 0)

    own_place = pl.multiple_of((2 * me + c) * R, R)
    value = tt[0]
    for way, buf in ((0, drl), (1, drr)):
        if way == 0 or kl:
            for h in range(2):
                hand_back(1, h, way).wait_recv()
            value = value + buf[0].astype(F32)
    gg[pl.ds(own_place, R), :] = value.astype(BF16)

    def share(j):
        dx, dy = j // ny, lax.rem(j, ny)
        rows = pl.ds(own_place, R)
        return pltpu.make_async_remote_copy(
            src_ref=gg.at[rows],
            dst_ref=gg.at[rows],
            send_sem=e_send.at[j],
            recv_sem=e_recv.at[me],
            device_id={"x": lax.rem(x + dx, nx), "y": lax.rem(y + dy, ny)},
            device_id_type=GRID,
        )

    def relay(q):
        rows = pl.ds(pl.multiple_of((2 * q + c) * R, R), R)
        return pltpu.make_async_remote_copy(
            src_ref=gg.at[rows],
            dst_ref=gg.at[rows],
            send_sem=f_send.at[q],
            recv_sem=f_recv.at[q],
            device_id=sibling,
            device_id_type=GRID,
        )

    def share_came(q):
        rows = pl.ds(pl.multiple_of((2 * q + c) * R, R), R)
        return pltpu.make_async_remote_copy(
            src_ref=gg.at[rows],
            dst_ref=gg.at[rows],
            send_sem=e_send.at[0],
            recv_sem=e_recv.at[q],
            device_id=sibling,
            device_id_type=GRID,
        )

    def relay_came(q):
        rows = pl.ds(pl.multiple_of((2 * q + 1 - c) * R, R), R)
        return pltpu.make_async_remote_copy(
            src_ref=gg.at[rows],
            dst_ref=gg.at[rows],
            send_sem=f_send.at[q],
            recv_sem=f_recv.at[q],
            device_id=sibling,
            device_id_type=GRID,
        )

    def start_share(j, _):
        share(j).start()
        return 0

    def start_relay(j, _):
        dx, dy = j // ny, lax.rem(j, ny)
        q = lax.rem(x + nx - dx, nx) * ny + lax.rem(y + ny - dy, ny)
        share_came(q).wait_recv()
        relay(q).start()
        return 0

    def end_relay(q, _):
        relay_came(q).wait_recv()
        return 0

    lax.fori_loop(1, chips, start_share, 0)
    relay(me).start()
    lax.fori_loop(1, chips, start_relay, 0)
    lax.fori_loop(0, chips, end_relay, 0)

    mine = pl.ds(pl.multiple_of(c * H, H), H)
    rest = pl.ds(pl.multiple_of((1 - c) * H, H), H)
    outs = []
    for i in range(T // chunk):
        rows = pl.ds(i * chunk, chunk)
        mixed = jnp.dot(cb[0, rows, :], gg[mine, :], preferred_element_type=F32)
        mixed = mixed + jnp.dot(cb[1, rows, :], gg[rest, :], preferred_element_type=F32)
        outv[rows, :] = (mixed * rinv[rows, 0:1]).astype(BF16)
        outs.append(pltpu.make_async_copy(outv.at[rows], mixed_hbm.at[rows], out_sem.at[i]))
        outs[-1].start()

    swap.wait_send()
    for xh, yt, ct, number in targets():
        for what in ("stat", "part"):
            here, far, near = to_owner(xh, yt, ct, number, what)
            pl.when(jnp.logical_not(here))(far.wait_send)

    def sent_gather(k, _):
        for h in range(2):
            pass_on(0, h, right, k).wait_send()

            @pl.when(k <= kl)
            def _():
                pass_on(0, h, left, kr + k).wait_send()

            hand_back(k, h, 0).wait_send()

            @pl.when(k <= kl)
            def _():
                hand_back(k, h, 1).wait_send()

        return 0

    def sent_share(j, _):
        share(j).wait_send()
        return 0

    def sent_relay(q, _):
        relay(q).wait_send()
        return 0

    lax.fori_loop(1, kr + 1, sent_gather, 0)
    lax.fori_loop(1, chips, sent_share, 0)
    lax.fori_loop(0, chips, sent_relay, 0)
    for out in outs:
        out.wait()


def body(sizes, tokens, slot_weight, expert_in, expert_out):
    nz, nx, ny = sizes
    first = jnp.swapaxes(expert_in, 1, 2)
    T, D = tokens.shape
    S = slot_weight.shape[1]
    H = S // 2
    chips = nx * ny
    R = S // (2 * chips)
    E, FF = first.shape[:2]
    kr = nz // 2
    vmem = pltpu.VMEM
    dma = pltpu.SemaphoreType.DMA
    anywhere = pl.BlockSpec(memory_space=pl.ANY)
    return pl.pallas_call(
        functools.partial(layer, sizes),
        out_shape=jax.ShapeDtypeStruct((T, D), BF16),
        in_specs=[anywhere] * 4,
        out_specs=anywhere,
        scratch_shapes=[
            vmem((T, D), BF16),
            vmem((2, D, H), BF16),
            vmem((E, FF, D), BF16),
            vmem((E, FF, D), BF16),
            vmem((2 * T, D), BF16),
            vmem((2 * T, H), F32),
            vmem((T, H), F32),
            vmem((2 * T, H), BF16),
            vmem((H, D), BF16),
            vmem((H // LANES, 8, LANES), F32),
            vmem((chips, R, D), BF16),
            vmem((chips, 8, LANES), F32),
            vmem((LANES, LANES), F32),
            vmem((nz, R, D), BF16),
            vmem((nz, R, D), F32),
            vmem((kr + 1, R, D), BF16),
            vmem((kr + 1, R, D), BF16),
            vmem((kr + 1, R, D), BF16),
            vmem((kr + 1, R, D), BF16),
            vmem((S, D), BF16),
            vmem((2, T, H), BF16),
            vmem((T, LANES), F32),
            vmem((T, D), BF16),
            dma((5,)),
            dma((T // min(256, T),)),
            dma((2,)),
            dma((chips,)),
            dma((chips,)),
            dma((chips,)),
            dma((chips,)),
            dma((nz, 2)),
            dma((nz, 2)),
            dma((2, kr + 1, 2)),
            dma((2, kr + 1, 2)),
            dma((chips,)),
            dma((chips,)),
            dma((chips,)),
            dma((chips,)),
        ],
        compiler_params=pltpu.CompilerParams(
            collective_id=0, has_side_effects=True, vmem_limit_bytes=56 * 2**20
        ),
        name="soft_moe",
    )(tokens, slot_weight, first, expert_out)


def build(devices, sizes):
    nz, nx, ny = sizes
    torus = Mesh(devices.reshape(nz, nx, ny, 2), ("z", "x", "y", "c"))
    token = ("x", "y", "c")
    rows = ("z", "x", "y", "c")
    placed = (P(rows, None), P(), P(token, None, "z"), P(token, "z", None))
    return jax.shard_map(
        functools.partial(body, sizes),
        mesh=torus,
        in_specs=placed,
        out_specs=P(rows, None),
        check_vma=False,
    )


def solution(mesh):
    return build(mesh.devices, (mesh.shape["batch"], 4, 4))
```

time: 177 us -> 106 us (0.60)
  blocking collectives: 137 us -> 0 us
  Pallas kernels: 0 us -> 104 us
  waiting for transfers between devices: 22.5 us -> 0 us
  matrix products: 8.2 us -> 0 us
  starting transfers between devices: 4.14 us -> 0 us
  other arithmetic: 2.79 us -> 0 us
    pallas_call x0 -> x1, Pallas kernels: none -> 104 us  [body(): pl.pallas_call(functools.partial(layer, sizes), out_shape=jax.ShapeDtypeS...]
    all_to_all x2 -> x0, blocking collectives: 74.1 us -> none  [the longest x1 38 us: from_everyone(): return lax.all_to_all(copies, axis, split_axis=0, concat_axis=0, tiled=True)]
    all_gather x4 -> x0, blocking collectives: 62.9 us -> none  [the longest x3 32.3 us: gathered_once(): both, at, found = (lax.all_gather(jnp.concatenate(lines), axis), 0, {})]
    all_to_all x1 -> x0, waiting for transfers between devices: 22.5 us -> none  [sent_and_summed(): lax.all_to_all(blocks, axis, split_axis=0, concat_axis=0, tiled=True)]
    dot_general x5 -> x0, matrix products: 8.2 us -> none  [the longest x1 2.27 us: body(): jnp.einsum('ts,td->sd', dispatch, normed, preferred_element_type=jnp.floa...]
    all_to_all x1 -> x0, starting transfers between devices: 4.14 us -> none  [sent_and_summed(): lax.all_to_all(blocks, axis, split_axis=0, concat_axis=0, tiled=True)]
    reduce_sum x4 -> x0, other arithmetic: 2.55 us -> none  [the longest x1 1.48 us: body(): jnp.mean(widened * widened, axis=-1, keepdims=True) + 1e-06]
  transfers between devices with their start and end apart: 1 -> 0, of which waited for: 1 -> 0; matrix products, arithmetic and copies ran while one was open for 0% -> 0% of each run, Pallas kernels for 0% -> 0%
where the time goes in v1:
time: 106 us
  Pallas kernels  104 us (98%)
  local copies, waits for them, and re-layouts  2.06 us (2%)
    pallas_call x1, Pallas kernels, body(): pl.pallas_call(functools.partial(layer, sizes), out_shape=jax.ShapeDtypeS...  104 us

profile of v1, /device:TPU:1, one launch (start us, length us, event | category | flops | bytes accessed | tf_op | source)
XLA Modules:
  0.0 106.0 jit_solution(4619271763602899404)
XLA Ops:
  0.0 104.0 %soft_moe.1 = bf16[512,768]{1,0:T(8,128)(2,1)} custom-call(bf16[512,768]{1,0:T(8,128)(2,1)} %tokens_hbm.1, bf16[768,1024]{1,0:T(8,128)(2,1)} %slot_hbm.1, bf16[4,192,768]{2,1,0:T(8,128)(2,1)} %bitcast.1, bf16[4,192,768]{2,1,0:T(8,128)(2,1)} %second_hbm.1), custom_call_target="tpu_custom_call" | custom-call | tf_op jit(solution)/shard_map/soft_moe/pallas_call | solution.py:498
  104.0 2.1 %copy.6 = bf16[512,768]{1,0:T(8,128)(2,1)} copy(bf16[512,768]{1,0:T(8,128)(2,1)} %soft_moe.1) | data formatting | bytes 1572864

commit v2 on v1

v2 whole, which is shorter than its diff:
```python
import functools

import jax
import jax.numpy as jnp
from jax import lax
from jax.experimental import pallas as pl
from jax.experimental.pallas import tpu as pltpu
from jax.sharding import Mesh
from jax.sharding import PartitionSpec as P

GRID = pl.DeviceIdType.MESH
F32 = jnp.float32
BF16 = jnp.bfloat16
LANES = 128
ORDER = (
    "B0", "B1", "G01", "G03", "X01", "G11", "G13", "G04", "G02", "G06", "X02", "L02", "X11", "G14",
    "G12", "G16", "G05", "X05", "G07", "G08", "X07", "L08", "L07", "L05", "X12", "G15", "X15", "L12",
    "L15", "G17", "G18", "X17", "L18", "L17", "L04", "L01", "L06", "L14", "L11", "L16", "L03", "L13",
    "R0", "R1",
)
BATCHES = {1: (1, 3), 2: (2, 4), 5: (5, 6), 7: (7, 8)}


def parent(r, top):
    if r % 3 == 0:
        return r - 3
    return r - 2 if r == top and r % 3 == 2 else r - 1


def layer(
    sizes,
    tokens_hbm,
    slot_hbm,
    first_hbm,
    second_hbm,
    mixed_hbm,
    tok,
    wv,
    w1,
    w2,
    nrm,
    lg,
    lo,
    dsp,
    part,
    st,
    rb,
    sr,
    vv,
    xin,
    tt,
    dsl,
    dsr,
    drl,
    drr,
    gg,
    cb,
    rinv,
    outv,
    total_out,
    load_sem,
    out_sem,
    tok_sem,
    st_send,
    st_recv,
    pb_send,
    pb_recv,
    c_send,
    c_recv,
    d_send,
    d_recv,
    e_send,
    e_recv,
    f_send,
    f_recv,
):
    nz, nx, ny = sizes
    z, x, y, c = (lax.axis_index(a) for a in ("z", "x", "y", "c"))
    T, D = tokens_hbm.shape
    S = slot_hbm.shape[1]
    H = S // 2
    E = first_hbm.shape[0]
    chips = nx * ny
    R = S // (2 * chips)
    RE = R // E
    xh_n = nx // 2
    kr = nz // 2
    kl = kr - 1
    me = x * ny + y
    half_rows = R // 2
    sibling = {"c": 1 - c}
    tops = (kr, kl)

    def along(way, step):
        return {"z": lax.rem(z + (step if way == 0 else nz - step), nz)}

    def halves(ref, i, h):
        return ref.at[i, pl.ds(h * half_rows, half_rows)]

    barrier = pltpu.get_barrier_semaphore()
    steps = sorted({r - parent(r, top) for top in tops for r in range(1, top + 1)})
    reach = sorted({d % nz for step in steps for d in (step, nz - step)})
    peers = len(reach)

    def greet(dev):
        pl.semaphore_signal(barrier, inc=1, device_id=dev, device_id_type=GRID)

    for step in reach:
        greet({"z": lax.rem(z + step, nz)})
    for dx in range(nx):
        for dy in range(ny):
            for dc in range(2):
                if dx or dy or dc:
                    greet(
                        {
                            "x": lax.rem(x + dx, nx),
                            "y": lax.rem(y + dy, ny),
                            "c": lax.rem(c + dc, 2),
                        }
                    )
                    peers += 1

    chunk = T // 2
    own_cols = pl.ds(pl.multiple_of(c * H, LANES), H)
    other_cols = pl.ds(pl.multiple_of((1 - c) * H, LANES), H)
    loads = [
        pltpu.make_async_copy(tokens_hbm.at[pl.ds(0, chunk)], tok.at[pl.ds(0, chunk)], load_sem.at[0]),
        pltpu.make_async_copy(slot_hbm.at[:, own_cols], wv.at[0], load_sem.at[1]),
        pltpu.make_async_copy(slot_hbm.at[:, other_cols], wv.at[1], load_sem.at[2]),
        pltpu.make_async_copy(first_hbm, w1, load_sem.at[3]),
        pltpu.make_async_copy(second_hbm, w2, load_sem.at[4]),
    ]
    later = pl.ds(chunk, chunk)
    loads.insert(1, pltpu.make_async_copy(tokens_hbm.at[later], tok.at[later], load_sem.at[5]))
    for load in loads:
        load.start()

    loads[0].wait()

    def normalize(i, _):
        rows = pl.ds(pl.multiple_of(i * 64, 64), 64)
        wide = tok[rows, :].astype(F32)
        mean = jnp.mean(wide * wide, axis=-1, keepdims=True)
        nrm[rows, :] = (wide * lax.rsqrt(mean + 1e-6)).astype(BF16)
        return 0

    lax.fori_loop(0, chunk // 64, normalize, 0)
    loads[1].wait()
    lax.fori_loop(chunk // 64, T // 64, normalize, 0)

    pl.semaphore_wait(barrier, peers)

    def swap(i):
        return pltpu.make_async_remote_copy(
            src_ref=nrm.at[pl.ds(i * chunk, chunk)],
            dst_ref=nrm.at[pl.ds(T + i * chunk, chunk)],
            send_sem=tok_sem.at[0, i],
            recv_sem=tok_sem.at[1, i],
            device_id=sibling,
            device_id_type=GRID,
        )

    for i in range(2):
        swap(i).start()

    loads[2].wait()
    loads[3].wait()
    for i in range(T // chunk):
        rows = pl.ds(i * chunk, chunk)
        lg[rows, :] = jnp.dot(nrm[rows, :], wv[0], preferred_element_type=F32)
        lo[rows, :] = jnp.dot(nrm[rows, :], wv[1], preferred_element_type=F32)
    for i in range(T // chunk):
        swap(i).wait_recv()
        rows = pl.ds(T + i * chunk, chunk)
        lg[rows, :] = jnp.dot(nrm[rows, :], wv[0], preferred_element_type=F32)

    step_rows = 64

    def highest(i, best):
        rows = pl.ds(pl.multiple_of(i * step_rows, step_rows), step_rows)
        block = lg[rows, :].reshape(step_rows // 8, 8, H)
        return jnp.maximum(best, jnp.max(block, axis=0))

    best = lax.fori_loop(0, 2 * T // step_rows, highest, jnp.full((8, H), -jnp.inf, F32))
    column_max = jnp.max(best, axis=0, keepdims=True)

    def raise_rows(i, total):
        rows = pl.ds(pl.multiple_of(i * step_rows, step_rows), step_rows)
        raised = jnp.exp(lg[rows, :] - column_max)
        dsp[rows, :] = raised.astype(BF16)
        return total + jnp.sum(raised.reshape(step_rows // 8, 8, H), axis=0)

    total = lax.fori_loop(0, 2 * T // step_rows, raise_rows, jnp.zeros((8, H), F32))
    column_sum = jnp.sum(total, axis=0, keepdims=True)
    for j in range(H // LANES):
        cols = slice(j * LANES, (j + 1) * LANES)
        st[j, 0:1, :] = column_max[:, cols]
        st[j, 1:2, :] = column_sum[:, cols]

    def targets():
        for xh in range(xh_n):
            for yt in range(ny):
                for ct in range(2):
                    yield xh, yt, ct, (xh * ny + yt) * 2 + ct

    def to_owner(xh, yt, ct, number, h):
        xt = xh_n * c + xh
        row = number * R
        if h is None:
            src, dst = st.at[row // LANES], sr.at[me]
            ssem, rsem = st_send.at[number], st_recv.at[me]
        else:
            src, dst = part.at[pl.ds(row + h * half_rows, half_rows)], halves(rb, me, h)
            ssem, rsem = pb_send.at[number, h], pb_recv.at[me, h]
        here = (xt == x) & (yt == y) & (ct == c)
        far = pltpu.make_async_remote_copy(
            src_ref=src,
            dst_ref=dst,
            send_sem=ssem,
            recv_sem=rsem,
            device_id={"x": xt, "y": yt, "c": ct},
            device_id_type=GRID,
        )
        near = pltpu.make_async_copy(src, dst, rsem)
        return here, far, near

    def start_owner(*args):
        here, far, near = to_owner(*args)
        pl.when(jnp.logical_not(here))(far.start)
        pl.when(here)(near.start)

    for target in targets():
        start_owner(*target, None)

    block = ny * 2 * R
    for xh in range(xh_n):
        value = lax.dot_general(
            dsp[:, xh * block : (xh + 1) * block],
            nrm[...],
            (((0,), (0,)), ((), ())),
            preferred_element_type=F32,
        )
        part[xh * block : (xh + 1) * block, :] = value.astype(BF16)
        for target in targets():
            if target[0] == xh:
                start_owner(*target, 0)
    for target in targets():
        start_owner(*target, 1)

    def combine_rows(i, _):
        rows = pl.ds(pl.multiple_of(i * 32, 32), 32)
        one, two = lg[rows, :], lo[rows, :]
        top = jnp.maximum(
            jnp.max(one, axis=1, keepdims=True), jnp.max(two, axis=1, keepdims=True)
        )
        one, two = jnp.exp(one - top), jnp.exp(two - top)
        for k in range(xh_n):
            part_k = slice(k * block, (k + 1) * block)
            cb[xh_n * c + k, rows, :] = one[:, part_k].astype(BF16)
            cb[xh_n * (1 - c) + k, rows, :] = two[:, part_k].astype(BF16)
        weight = jnp.sum(one, axis=1, keepdims=True) + jnp.sum(two, axis=1, keepdims=True)
        rinv[rows, :] = jnp.broadcast_to(1.0 / weight, (32, LANES))
        return 0

    lax.fori_loop(0, T // 32, combine_rows, 0)

    def arrived(ref, sem):
        return pltpu.make_async_remote_copy(
            src_ref=ref,
            dst_ref=ref,
            send_sem=sem,
            recv_sem=sem,
            device_id=sibling,
            device_id_type=GRID,
        )

    for q in range(chips):
        arrived(sr.at[q], st_recv.at[q]).wait_recv()
    highs = [sr[q, 0:1, :] for q in range(chips)]
    peak = functools.reduce(jnp.maximum, highs)
    weights = [jnp.exp(t - peak) for t in highs]
    sums = functools.reduce(jnp.add, [w * sr[q, 1:2, :] for q, w in enumerate(weights)])
    vv[...] = jnp.zeros_like(vv)
    for q in range(chips):
        vv[q : q + 1, :] = weights[q] / sums
    vv[...] = jnp.transpose(vv[...])
    offset = lax.rem((lax.rem(x, xh_n) * ny + y) * 2 * R + c * R, LANES)

    def place(way, r):
        return 0 if r == 0 else way * kr + r

    def children(way, r):
        top = tops[way]
        return sorted((k for k in range(1, top + 1) if parent(k, top) == r), reverse=True)

    def pass_on(way, r, to, h):
        return pltpu.make_async_remote_copy(
            src_ref=halves(xin, place(way, r), h),
            dst_ref=halves(xin, place(way, to), h),
            send_sem=c_send.at[place(way, to), h],
            recv_sem=c_recv.at[place(way, to), h],
            device_id=along(way, to - r),
            device_id_type=GRID,
        )

    def owner_sum(h):
        rows = pl.ds(h * half_rows, half_rows)
        scale = vv[pl.ds(pl.multiple_of(offset + h * half_rows, half_rows), half_rows), :]
        acc = jnp.zeros((half_rows, D), F32)
        for q in range(chips):
            arrived(halves(rb, q, h), pb_recv.at[q, h]).wait_recv()
            acc = acc + scale[:, q : q + 1] * rb[q, rows, :].astype(F32)
        xin[0, rows, :] = acc.astype(BF16)
        forward(0, h)

    def forward(r, h):
        edges = [(to, way) for way in range(2) for to in children(way, r)]
        for to, way in sorted(edges, reverse=True):
            pass_on(way, r, to, h).start()

    def gather(r, h):
        for way in range(2):
            if r <= tops[way]:
                pass_on(way, parent(r, tops[way]), r, h).wait_recv()
                for to in children(way, r):
                    pass_on(way, r, to, h).start()

    def experts(first, h):
        spots = []
        for r in BATCHES[first]:
            if r <= kr:
                spots += [r, kr + r if r <= kl else 0]
        rows = pl.ds(h * half_rows, half_rows)
        blocks = [xin[spot, rows, :].astype(F32) for spot in spots]
        for i in range(E // 2):
            e = h * (E // 2) + i
            mine = slice(i * RE, (i + 1) * RE)
            lhs = jnp.concatenate([block[mine] for block in blocks], axis=0).astype(BF16)
            hidden = lax.dot_general(
                lhs, w1[e], (((1,), (1,)), ((), ())), preferred_element_type=F32
            )
            hidden = 0.5 * hidden * (1.0 + lax.erf(hidden * (0.5**0.5)))
            terms = jnp.dot(hidden.astype(BF16), w2[e], preferred_element_type=F32)
            for n, spot in enumerate(spots):
                tt[spot, pl.ds(e * RE, RE), :] = terms[n * RE : (n + 1) * RE]

    def hand_back(way, r, h):
        src, dst = ((dsl, drl), (dsr, drr))[way]
        return pltpu.make_async_remote_copy(
            src_ref=halves(src, r, h),
            dst_ref=halves(dst, r, h),
            send_sem=d_send.at[way, r, h],
            recv_sem=d_recv.at[way, r, h],
            device_id=along(1 - way, r - parent(r, tops[way])),
            device_id_type=GRID,
        )

    def summed(way, r, h, value):
        rows = pl.ds(h * half_rows, half_rows)
        for k in reversed(children(way, r)):
            hand_back(way, k, h).wait_recv()
            value = value + (drl, drr)[way][k, rows, :].astype(F32)
        return value

    def give_back(r, h):
        rows = pl.ds(h * half_rows, half_rows)
        for way in range(2):
            if r <= tops[way]:
                value = summed(way, r, h, tt[place(way, r), rows, :])
                (dsl, dsr)[way][r, rows, :] = value.astype(BF16)
                hand_back(way, r, h).start()

    own_place = pl.multiple_of((2 * me + c) * R, R)

    def result(h):
        value = tt[0, pl.ds(h * half_rows, half_rows), :]
        for way in range(2):
            value = summed(way, 0, h, value)
        start = pl.multiple_of(own_place + h * half_rows, half_rows)
        gg[pl.ds(start, half_rows), :] = value.astype(BF16)
        relay(me, h).start()

        def start_share(i, _):
            share(far_first(i), h).start()
            return 0

        lax.fori_loop(1, chips, start_share, 0)

    def half_of(q, core, h):
        return gg.at[pl.ds(pl.multiple_of((2 * q + core) * R + h * half_rows, half_rows), half_rows)]

    def share(j, h):
        dx, dy = j // ny, lax.rem(j, ny)
        ref = half_of(me, c, h)
        return pltpu.make_async_remote_copy(
            src_ref=ref,
            dst_ref=ref,
            send_sem=e_send.at[j, h],
            recv_sem=e_recv.at[me, h],
            device_id={"x": lax.rem(x + dx, nx), "y": lax.rem(y + dy, ny)},
            device_id_type=GRID,
        )

    def relay(q, h):
        ref = half_of(q, c, h)
        return pltpu.make_async_remote_copy(
            src_ref=ref,
            dst_ref=ref,
            send_sem=f_send.at[q, h],
            recv_sem=f_recv.at[q, h],
            device_id=sibling,
            device_id_type=GRID,
        )

    def far_first(i):
        dx = i // ny
        mid = nx // 2
        dx = jnp.where(dx < mid, dx, jnp.where(dx == nx - 1, mid, dx + 1))
        return dx * ny + lax.rem(i, ny)

    def from_chip(j):
        dx, dy = j // ny, lax.rem(j, ny)
        return lax.rem(x + nx - dx, nx) * ny + lax.rem(y + ny - dy, ny)

    def relay_row(row, h):
        def start_relay(i, _):
            q = from_chip(far_first(i))
            arrived(half_of(q, c, h), e_recv.at[q, h]).wait_recv()
            relay(q, h).start()
            return 0

        lax.fori_loop(max(1, row * ny), (row + 1) * ny, start_relay, 0)

    def row_came(row, h):
        def end_relay(i, _):
            q = from_chip(far_first(i))
            arrived(half_of(q, 1 - c, h), f_recv.at[q, h]).wait_recv()
            return 0

        lax.fori_loop(row * ny, (row + 1) * ny, end_relay, 0)

    loads[4].wait()
    loads[5].wait()
    acts = dict(
        B=lambda _, h: owner_sum(h),
        G=gather,
        X=experts,
        L=give_back,
        R=lambda _, h: result(h),
    )
    for step in ORDER:
        kind, h, r = step[0], int(step[1]), int(step[2:] or 0)
        if r <= kr:
            acts[kind](r, h)

    def mix(row, last_row):
        xt = lax.rem(x + nx - far_first(row * ny) // ny, nx)
        places = pl.ds(pl.multiple_of(xt * block, block), block)
        for i in range(T // chunk):
            rows = pl.ds(i * chunk, chunk)
            value = jnp.dot(cb[xt, rows, :], gg[places, :], preferred_element_type=F32)
            if row:
                value = value + total_out[rows, :]
            if last_row:
                outv[rows, :] = (value * rinv[rows, 0:1]).astype(BF16)
                write_out(i).start()
            else:
                total_out[rows, :] = value

    def write_out(i):
        rows = pl.ds(i * chunk, chunk)
        return pltpu.make_async_copy(outv.at[rows], mixed_hbm.at[rows], out_sem.at[i])

    for row in range(nx):
        for h in range(2):
            relay_row(row, h)
        if row:
            for h in range(2):
                row_came(row - 1, h)
            mix(row - 1, False)
    for h in range(2):
        row_came(nx - 1, h)
    mix(nx - 1, True)

    for i in range(2):
        swap(i).wait_send()
    for target in targets():
        for h in (None, 0, 1):
            here, far, near = to_owner(*target, h)
            pl.when(jnp.logical_not(here))(far.wait_send)
    for way in range(2):
        for r in range(1, tops[way] + 1):
            for h in range(2):
                pass_on(way, parent(r, tops[way]), r, h).wait_send()
                hand_back(way, r, h).wait_send()
    for h in range(2):

        def sent_share(j, _):
            share(j, h).wait_send()
            return 0

        def sent_relay(q, _):
            relay(q, h).wait_send()
            return 0

        lax.fori_loop(1, chips, sent_share, 0)
        lax.fori_loop(0, chips, sent_relay, 0)
    for i in range(T // chunk):
        write_out(i).wait()


def body(sizes, tokens, slot_weight, expert_in, expert_out):
    nz, nx, ny = sizes
    first = jnp.swapaxes(expert_in, 1, 2)
    T, D = tokens.shape
    S = slot_weight.shape[1]
    H = S // 2
    chips = nx * ny
    R = S // (2 * chips)
    E, FF = first.shape[:2]
    kr = nz // 2
    arrays = (tokens, slot_weight, first, expert_out)
    vmem = pltpu.VMEM
    dma = pltpu.SemaphoreType.DMA
    anywhere = pl.BlockSpec(memory_space=pl.ANY)
    return pl.pallas_call(
        functools.partial(layer, sizes),
        out_shape=jax.ShapeDtypeStruct((T, D), BF16),
        in_specs=[pl.BlockSpec(memory_space=pltpu.HBM)] * 4,
        out_specs=anywhere,
        scratch_shapes=[
            vmem((T, D), BF16),
            vmem((2, D, H), BF16),
            vmem((E, FF, D), BF16),
            vmem((E, FF, D), BF16),
            vmem((2 * T, D), BF16),
            vmem((2 * T, H), F32),
            vmem((T, H), F32),
            vmem((2 * T, H), BF16),
            vmem((H, D), BF16),
            vmem((H // LANES, 8, LANES), F32),
            vmem((chips, R, D), BF16),
            vmem((chips, 8, LANES), F32),
            vmem((LANES, LANES), F32),
            vmem((nz, R, D), BF16),
            vmem((nz, R, D), F32),
            vmem((kr + 1, R, D), BF16),
            vmem((kr + 1, R, D), BF16),
            vmem((kr + 1, R, D), BF16),
            vmem((kr + 1, R, D), BF16),
            vmem((S, D), BF16),
            vmem((nx, T, ny * 2 * R), BF16),
            vmem((T, LANES), F32),
            vmem((T, D), BF16),
            vmem((T, D), F32),
            dma((6,)),
            dma((2,)),
            dma((2, 2)),
            dma((chips,)),
            dma((chips,)),
            dma((chips, 2)),
            dma((chips, 2)),
            dma((nz, 2)),
            dma((nz, 2)),
            dma((2, kr + 1, 2)),
            dma((2, kr + 1, 2)),
            dma((chips, 2)),
            dma((chips, 2)),
            dma((chips, 2)),
            dma((chips, 2)),
        ],
        compiler_params=pltpu.CompilerParams(
            collective_id=0, has_side_effects=True, vmem_limit_bytes=28 * 2**20
        ),
        name="soft_moe",
    )(*(pltpu.with_memory_space_constraint(a, pltpu.HBM) for a in arrays))


def build(devices, sizes):
    nz, nx, ny = sizes
    torus = Mesh(devices.reshape(nz, nx, ny, 2), ("z", "x", "y", "c"))
    token = ("x", "y", "c")
    rows = ("z", "x", "y", "c")
    placed = (P(rows, None), P(), P(token, None, "z"), P(token, "z", None))
    return jax.shard_map(
        functools.partial(body, sizes),
        mesh=torus,
        in_specs=placed,
        out_specs=P(rows, None),
        check_vma=False,
    )


def solution(mesh):
    return build(mesh.devices, (mesh.shape["batch"], 4, 4))
```

time: 106 us -> 80.5 us (0.76)
  Pallas kernels: 104 us -> 79.5 us
  local copies, waits for them, and re-layouts: 2.06 us -> 0.88 us
    pallas_call x1, Pallas kernels: 104 us -> 79.5 us  [body(): pl.pallas_call(functools.partial(layer, sizes), out_shape=jax.ShapeDtypeS...]
    unnamed x1, local copies, waits for them, and re-layouts: 2.06 us -> 0.88 us
where the time goes in v2:
time: 80.5 us; the launch traced here: 80.4 us
  Pallas kernels  79.5 us (99%)
  local copies, waits for them, and re-layouts  0.88 us (1%)
    pallas_call x1, Pallas kernels, body(): pl.pallas_call(functools.partial(layer, sizes), out_shape=jax.ShapeDtypeS...  79.5 us

profile of v2, /device:TPU:1, one launch (start us, length us, event | category | flops | bytes accessed | tf_op | source)
XLA Modules:
  0.0 80.4 jit_solution(5255843612834994628)
XLA Ops:
  0.0 79.5 %soft_moe.1 = bf16[512,768]{1,0:T(8,128)(2,1)S(1)} custom-call(bf16[512,768]{1,0:T(8,128)(2,1)} %tokens_hbm.1, bf16[768,1024]{1,0:T(8,128)(2,1)} %slot_hbm.1, bf16[4,192,768]{2,1,0:T(8,128)(2,1)} %bitcast.1, bf16[4,192,768]{2,1,0:T(8,128)(2,1)} %second_hbm.1), custom_call_target="tpu_custom_call" | custom-call | tf_op jit(solution)/shard_map/soft_moe/pallas_call | solution.py:526
  79.5 0.9 %copy.6 = bf16[512,768]{1,0:T(8,128)(2,1)} copy(bf16[512,768]{1,0:T(8,128)(2,1)S(1)} %soft_moe.1) | data formatting | bytes 1572864
